TPU v7x, 32 devices: a whole 2x2x4 slice. The times are simulated.
32 devices in a mesh: dp: 4 (over z), ctx: 4 (over y, x), tensor: 2 (over core).
Axes of the slice: x: 2, y: 2, z: 4, core: 2. Of those that a mesh axis runs over, the one named last changes fastest.
Arguments:
- tokens: bfloat16 [4096, 1024], P(('dp', 'ctx')), may hold values from -6 to 6
- doc_lengths: int32 [4, 8], P('dp'), may hold values from 1 to 512, 1024 in all within a row
- gain_attn: bfloat16 [1024], P('dp'), may hold values from 0.5 to 1.5
- w_qkv: bfloat16 [3, 1024, 1024], P(None, 'dp', 'tensor'), may hold values from -0.1875 to 0.1875
- w_attn_out: bfloat16 [1024, 1024], P('tensor', 'dp'), may hold values from -0.5 to 0.5
- gain_mlp: bfloat16 [1024], P('dp'), may hold values from 0.5 to 1.5
- w_in: bfloat16 [2, 1024, 2624], P(None, 'dp', 'tensor'), may hold values from -0.1875 to 0.1875
- w_mlp_out: bfloat16 [2624, 1024], P('tensor', 'dp'), may hold values from -0.125 to 0.125
- cotangent: bfloat16 [4096, 1024], P(('dp', 'ctx')), may hold values from -6 to 6
Outputs:
- out_tokens: bfloat16 [4096, 1024], P(('dp', 'ctx'))
- grad_tokens: float32 [4096, 1024], P(('dp', 'ctx'))
- grad_gain_attn: float32 [1024], P('dp')
- grad_w_qkv: float32 [3, 1024, 1024], P(None, 'dp', 'tensor')
- grad_w_attn_out: float32 [1024, 1024], P('tensor', 'dp')
- grad_gain_mlp: float32 [1024], P('dp')
- grad_w_in: float32 [2, 1024, 2624], P(None, 'dp', 'tensor')
- grad_w_mlp_out: float32 [2624, 1024], P('tensor', 'dp')
Inputs may be any that keep to these rules, and one draw needn't show every extreme that they name: `doc_lengths`: each row sums to 1024, and the longest document of each row has exactly half of 1024 tokens.
All inputs are finite; a program needn't handle non-finite values.
Results may differ from a plain program's by a relative error of at most 0.013.
Values may be sent and summed in bfloat16 or wider, within the bound.
A program may use at most 128 MiB of HBM per device.

v0:
```python
import math
import jax
import jax.numpy as jnp
from jax import lax
from jax.sharding import PartitionSpec as P

HD = 64
NORM_EPS = 1e-05
ROPE_BASE = 160000.0
MASK_FILL = -1e30
INV_ROOT_TWO = 1.0 / math.sqrt(2.0)
INV_ROOT_TWO_PI = 1.0 / math.sqrt(2.0 * math.pi)


def norm_forward(x_float, gain_vec):
    row_mean = jnp.mean(x_float, axis=-1, keepdims=True)
    centered = x_float - row_mean
    inv_std = lax.rsqrt(jnp.mean(centered * centered, axis=-1, keepdims=True) + NORM_EPS)
    x_hat = centered * inv_std
    normed = (x_hat * gain_vec.astype(jnp.float32)).astype(jnp.bfloat16)
    return (x_hat, inv_std, normed)


def norm_backward(grad_out, x_hat, inv_std, gain_vec):
    grad_hat = grad_out * gain_vec.astype(jnp.float32)
    grad_gain = jnp.sum(grad_out * x_hat, axis=0)
    inner_term = (
        grad_hat
        - jnp.mean(grad_hat, axis=-1, keepdims=True)
        - x_hat * jnp.mean(grad_hat * x_hat, axis=-1, keepdims=True)
    )
    return (inv_std * inner_term, grad_gain)


def rope_tables(doc_len, span_len, head_width):
    doc_end = jnp.cumsum(doc_len)
    doc_start = doc_end - doc_len
    places = jnp.arange(span_len, dtype=jnp.int32)
    inside = places[:, None] >= doc_start[None, :]
    begins = jnp.max(jnp.where(inside, doc_start[None, :], 0), axis=1)
    segment = jnp.sum((places[:, None] >= doc_end[None, :]).astype(jnp.int32), axis=1)
    offset = (places - begins).astype(jnp.float32)
    half_width = head_width // 2
    frequency = ROPE_BASE ** (-(jnp.arange(half_width, dtype=jnp.float32) * (2.0 / head_width)))
    angles = offset[:, None] * frequency[None, :]
    angles = jnp.concatenate([angles, angles], axis=1)
    return (jnp.cos(angles), jnp.sin(angles), segment)


def rotate(values_in, cosines, sines):
    half_width = values_in.shape[-1] // 2
    turned = jnp.concatenate([-values_in[..., half_width:], values_in[..., :half_width]], axis=-1)
    return values_in * cosines[:, None, :] + turned * sines[:, None, :]


def rotate_back(grads_in, cosines, sines):
    half_width = grads_in.shape[-1] // 2
    scaled = grads_in * sines[:, None, :]
    turned = jnp.concatenate([scaled[..., half_width:], -scaled[..., :half_width]], axis=-1)
    return grads_in * cosines[:, None, :] + turned


def masked_scores(query_blk, keys_all, same_doc):
    score_scale = query_blk.shape[-1] ** (-0.5)
    scores = (
        jnp.einsum("bhe,che->hbc", query_blk, keys_all, preferred_element_type=jnp.float32)
        * score_scale
    )
    return jnp.where(same_doc[None, :, :], scores, MASK_FILL)


def attend_rows(query_blk, keys_all, vals_all, same_doc):
    scores = masked_scores(query_blk, keys_all, same_doc)
    row_max = jnp.max(scores, axis=-1, keepdims=True)
    expo_vals = jnp.exp(scores - row_max)
    row_total = jnp.sum(expo_vals, axis=-1, keepdims=True)
    prob_b = (expo_vals / row_total).astype(jnp.bfloat16)
    out_rows = jnp.einsum("hbc,che->bhe", prob_b, vals_all, preferred_element_type=jnp.float32)
    log_total = (row_max + jnp.log(row_total))[:, :, 0]
    return (out_rows.astype(jnp.bfloat16), log_total)


def attend_rows_back(query_blk, out_blk, grad_blk, log_blk, keys_all, vals_all, same_doc):
    score_scale = query_blk.shape[-1] ** (-0.5)
    scores = masked_scores(query_blk, keys_all, same_doc)
    probs = jnp.exp(scores - log_blk[:, :, None])
    prob_b = probs.astype(jnp.bfloat16)
    grad_vals = jnp.einsum("hbc,bhe->che", prob_b, grad_blk, preferred_element_type=jnp.float32)
    grad_prob = jnp.einsum("bhe,che->hbc", grad_blk, vals_all, preferred_element_type=jnp.float32)
    delta_row = jnp.sum(grad_blk.astype(jnp.float32) * out_blk.astype(jnp.float32), axis=-1).T
    grad_score = (probs * (grad_prob - delta_row[:, :, None]) * score_scale).astype(jnp.bfloat16)
    grad_query = jnp.einsum(
        "hbc,che->bhe", grad_score, keys_all, preferred_element_type=jnp.float32
    )
    grad_keys = jnp.einsum(
        "hbc,bhe->che", grad_score, query_blk, preferred_element_type=jnp.float32
    )
    return (grad_query, grad_keys, grad_vals)


BOTH = ("dp", "ctx")


def add_pair(part):
    part_b = part.astype(jnp.bfloat16)
    ways = lax.axis_size("tensor")
    total = part_b.astype(jnp.float32)
    for step in range(1, ways):
        pairs = [(src, (src + step) % ways) for src in range(ways)]
        total = total + lax.ppermute(part_b, "tensor", pairs).astype(jnp.float32)
    return total


def own_rows(block, axis):
    ways = lax.axis_size("ctx")
    rows = block.shape[axis] // ways
    return lax.dynamic_slice_in_dim(block, lax.axis_index("ctx") * rows, rows, axis)


def local(tokens, doc_lengths, gain_attn, w_qkv, w_attn_out, gain_mlp, w_in, w_mlp_out, cotangent):
    f32 = jnp.float32
    bf16 = jnp.bfloat16
    gains = lax.all_gather(jnp.stack([gain_attn, gain_mlp]), "dp", axis=1, tiled=True)
    gain_one, gain_two = (gains[0], gains[1])
    w_query_all = lax.all_gather(own_rows(w_qkv, 1), BOTH, axis=1, tiled=True)
    w_out_all = lax.all_gather(own_rows(w_attn_out.T, 0), BOTH, axis=0, tiled=True)
    w_in_all = lax.all_gather(own_rows(w_in, 1), BOTH, axis=1, tiled=True)
    w_down_all = lax.all_gather(own_rows(w_mlp_out.T, 0), BOTH, axis=0, tiled=True)
    ctx_ways = lax.axis_size("ctx")
    tok_rows = tokens.shape[0]
    span_len = tok_rows * ctx_ways
    local_width = w_query_all.shape[2]
    per_group = local_width // ctx_ways
    heads_here = per_group // HD
    cosines, sines, segment = rope_tables(doc_lengths[0], span_len, HD)
    same_doc = segment[:, None] == segment[None, :]
    x_float = tokens.astype(f32)
    hat_one, inv_one, normed_one = norm_forward(x_float, gain_one)
    projected = jnp.einsum(
        "td,kde->kte", normed_one, w_query_all, preferred_element_type=f32
    ).astype(bf16)
    projected = projected.reshape(3, tok_rows, ctx_ways, per_group)
    spread = lax.all_to_all(projected, "ctx", split_axis=2, concat_axis=1, tiled=True)
    spread = spread.reshape(3, span_len, heads_here, HD)
    query_rot = rotate(spread[0].astype(f32), cosines, sines).astype(bf16)
    keys_all = rotate(spread[1].astype(f32), cosines, sines).astype(bf16)
    vals_all = spread[2]
    attn_heads, log_rows = attend_rows(query_rot, keys_all, vals_all, same_doc)
    returned = lax.all_to_all(
        attn_heads.reshape(span_len, 1, per_group), "ctx", split_axis=0, concat_axis=1, tiled=True
    )
    attn_flat = returned.reshape(tok_rows, local_width)
    attn_total = add_pair(jnp.einsum("te,de->td", attn_flat, w_out_all, preferred_element_type=f32))
    mixed_one = x_float + attn_total
    hat_two, inv_two, normed_two = norm_forward(mixed_one, gain_two)
    pair_in = jnp.einsum("td,kde->kte", normed_two, w_in_all, preferred_element_type=f32)
    act_in = pair_in[0]
    gate_in = pair_in[1]
    cdf_val = 0.5 * (1.0 + jax.scipy.special.erf(act_in * INV_ROOT_TWO))
    gelu_val = act_in * cdf_val
    hidden = (gelu_val * gate_in).astype(bf16)
    mlp_total = add_pair(jnp.einsum("tf,df->td", hidden, w_down_all, preferred_element_type=f32))
    result = (mixed_one + mlp_total).astype(bf16)
    cot_float = cotangent.astype(f32)
    grad_mlp_out = jnp.einsum("td,tf->df", cotangent, hidden, preferred_element_type=f32)
    share_down = lax.psum_scatter(grad_mlp_out.astype(bf16), BOTH, scatter_dimension=0, tiled=True)
    grad_hidden = jnp.einsum("td,df->tf", cotangent, w_down_all, preferred_element_type=f32)
    gelu_slope = cdf_val + act_in * jnp.exp(-0.5 * act_in * act_in) * INV_ROOT_TWO_PI
    grad_pair = jnp.stack(
        [(grad_hidden * gate_in * gelu_slope).astype(bf16), (grad_hidden * gelu_val).astype(bf16)]
    )
    grad_in = [
        jnp.einsum("td,te->de", normed_two, grad_pair[k], preferred_element_type=f32)
        for k in range(2)
    ]
    share_in = [
        lax.psum_scatter(grad_in[k].astype(bf16), BOTH, scatter_dimension=0, tiled=True)
        for k in range(2)
    ]
    grad_normed_two = add_pair(
        jnp.einsum("kte,kde->td", grad_pair, w_in_all, preferred_element_type=f32)
    )
    back_two, grad_gain_mlp = norm_backward(grad_normed_two, hat_two, inv_two, gain_two)
    grad_mixed = cot_float + back_two
    grad_mixed_b = grad_mixed.astype(bf16)
    grad_attn_out = jnp.einsum("td,te->de", grad_mixed_b, attn_flat, preferred_element_type=f32)
    share_out = lax.psum_scatter(grad_attn_out.astype(bf16), BOTH, scatter_dimension=0, tiled=True)
    grad_local = jnp.einsum(
        "td,de->te", grad_mixed_b, w_out_all, preferred_element_type=f32
    ).astype(bf16)
    grad_spread = lax.all_to_all(
        grad_local.reshape(tok_rows, ctx_ways, per_group),
        "ctx",
        split_axis=1,
        concat_axis=0,
        tiled=True,
    )
    grad_heads = grad_spread.reshape(span_len, heads_here, HD)
    grad_query, grad_keys, grad_vals = attend_rows_back(
        query_rot, attn_heads, grad_heads, log_rows, keys_all, vals_all, same_doc
    )
    grad_query = rotate_back(grad_query, cosines, sines).astype(bf16)
    grad_keys = rotate_back(grad_keys, cosines, sines).astype(bf16)
    grad_stack = jnp.stack([grad_query, grad_keys, grad_vals.astype(bf16)]).reshape(
        3, span_len, 1, per_group
    )
    grad_back = lax.all_to_all(grad_stack, "ctx", split_axis=1, concat_axis=2, tiled=True)
    grad_proj = grad_back.reshape(3, tok_rows, local_width)
    grad_qkv = [
        jnp.einsum("td,te->de", normed_one, grad_proj[k], preferred_element_type=f32)
        for k in range(3)
    ]
    share_qkv = lax.psum_scatter(
        jnp.concatenate(grad_qkv, axis=1).astype(bf16), BOTH, scatter_dimension=0, tiled=True
    )
    share_qkv = share_qkv.reshape(-1, 3, local_width).transpose(1, 0, 2)
    grad_normed_one = add_pair(
        jnp.einsum("kte,kde->td", grad_proj, w_query_all, preferred_element_type=f32)
    )
    back_one, grad_gain_attn = norm_backward(grad_normed_one, hat_one, inv_one, gain_one)
    grad_tok = grad_mixed + back_one
    gain_sums = lax.psum(jnp.stack([grad_gain_attn, grad_gain_mlp]), BOTH)
    gain_rows = gain_attn.shape[0]
    gain_own = lax.dynamic_slice_in_dim(gain_sums, lax.axis_index("dp") * gain_rows, gain_rows, 1)
    own_down = lax.all_gather(share_down, "ctx", axis=0, tiled=True).astype(f32).T
    own_in = lax.all_gather(jnp.stack(share_in), "ctx", axis=1, tiled=True).astype(f32)
    own_out = lax.all_gather(share_out, "ctx", axis=0, tiled=True).astype(f32).T
    own_qkv = lax.all_gather(share_qkv, "ctx", axis=1, tiled=True).astype(f32)
    return (result, grad_tok, gain_own[0], own_qkv, own_out, gain_own[1], own_in, own_down)


def solution(mesh):
    in_specs = (
        P(("dp", "ctx"), None),
        P("dp", None),
        P("dp"),
        P(None, "dp", "tensor"),
        P("tensor", "dp"),
        P("dp"),
        P(None, "dp", "tensor"),
        P("tensor", "dp"),
        P(("dp", "ctx"), None),
    )
    out_specs = (
        P(("dp", "ctx"), None),
        P(("dp", "ctx"), None),
        P("dp"),
        P(None, "dp", "tensor"),
        P("tensor", "dp"),
        P("dp"),
        P(None, "dp", "tensor"),
        P("tensor", "dp"),
    )
    return jax.shard_map(local, mesh=mesh, in_specs=in_specs, out_specs=out_specs, check_vma=False)
```

profile of v0, /device:TPU:0, one launch (start us, length us, event | category | flops | bytes accessed | tf_op | source)
XLA Modules:
  0.0 824.5 jit_solution(13252264614928242169)
XLA Ops:
  7.3 1.8 constant_dynamic-slice_fusion.4
  14.1 12.7 %all_gather.28 = bf16[2,1024]{1,0:T(2,128)(2,1)S(1)} all-gather(bf16[2,256]{1,0:T(2,128)(2,1)S(1)} %pad_maximum_fusion.5), channel_id=1, replica_groups=mesh['dp'=4,'ctx'=4,'tensor'=2] {'dp'}, dimensions={1}, use_global_device_ids=true | all-gather | bytes 5120 | tf_op jit(solution)/shard_map/all_gather | solution.py:123
  26.9 55.1 %all-gather.6.cloned.1.call-done = bf16[3,1024,512]{2,1,0:T(8,128)(2,1)} async-done(((bf16[3,64,512]{2,1,0:T(8,128)(2,1)}), bf16[3,1024,512]{2,1,0:T(8,128)(2,1)}) %all-gather.6.cloned.1.call-update) | async-done | bytes 3145744 | tf_op jit(solution)/shard_map/all_gather | solution.py:125
  82.0 3.0 convolution_convert_fusion.7
  85.9 3.5 all-to-all-start
  91.2 7.8 all-to-all-done
  100.7 2.2 copy.172
  105.7 2.9 fusion.2
  108.6 2.0 fusion
  110.7 2.8 fusion.27
  115.1 8.7 %all_to_all.60 = bf16[4,2,16384]{2,1,0:T(2,128)(2,1)S(1)} all-to-all(bf16[4,2,16384]{2,1,0:T(2,128)(2,1)S(1)} %reshape.237), channel_id=1, replica_groups=mesh['dp'=4,'ctx'=4,'tensor'=2] {'ctx'}, dimensions={0} | all-to-all | bytes 524288 | tf_op jit(solution)/shard_map/all_to_all | solution.py:149
  124.3 17.6 %all-gather.8.cloned.1.call-done = bf16[1024,512]{1,0:T(8,128)(2,1)} async-done(((bf16[64,512]{1,0:T(8,128)(2,1)}), bf16[1024,512]{1,0:T(8,128)(2,1)}) %all-gather.8.cloned.1.call-update) | async-done | bytes 1048592 | tf_op jit(solution)/shard_map/all_gather | solution.py:126
  141.8 1.7 convolution_convert_fusion.8
  143.6 1.9 collective-permute-done
  146.1 86.8 %all-gather.10.cloned.1.call-done = bf16[2,1024,1312]{2,1,0:T(8,128)(2,1)} async-done(((bf16[2,64,1312]{2,1,0:T(8,128)(2,1)}), bf16[2,1024,1312]{2,1,0:T(8,128)(2,1)}) %all-gather.10.cloned.1.call-update) | async-done | bytes 5373968 | tf_op jit(solution)/shard_map/all_gather | solution.py:127
  232.8 6.0 convolution_bitcast_fusion
  238.9 61.3 %all-gather.12.cloned.1.call-done = bf16[1024,1312]{1,0:T(8,128)(2,1)} async-done(((bf16[64,1312]{1,0:T(8,128)(2,1)}), bf16[1024,1312]{1,0:T(8,128)(2,1)}) %all-gather.12.cloned.1.call-update) | async-done | bytes 2686992 | tf_op jit(solution)/shard_map/all_gather | solution.py:128
  300.2 4.9 fusion.13
  305.9 2.7 convolution_convert_fusion.2
  308.7 3.9 convolution_convert_fusion.1
  312.6 5.0 fusion.17
  323.1 1.5 convolution_convert_fusion.6
  324.8 2.1 fusion.7
  326.9 2.9 copy.207
  331.1 1.7 convolution_convert_fusion.10
  333.6 3.4 all-to-all-start.2
  337.1 9.5 %all-to-all-done.2 = bf16[256,4,128]{0,2,1:T(8,128)(2,1)S(1)} async-done(((bf16[256,4,128]{0,2,1:T(8,128)(2,1)}), bf16[256,4,128]{0,2,1:T(8,128)(2,1)S(1)}, u32[]{:S(2)}, u32[]{:S(2)}) %all-to-all-start.2) | async-done | bytes 262176 | tf_op jit(solution)/shard_map/all_to_all | solution.py:191
  347.0 6.6 fusion.28
  356.1 6.8 multiply_convert_fusion
  367.7 23.4 %reduce-scatter.12.cloned.1.call-done = bf16[64,1312]{1,0:T(8,128)(2,1)} async-done(((bf16[1024,1312]{1,0:T(8,128)(2,1)}), bf16[64,1312]{1,0:T(8,128)(2,1)}) %reduce-scatter.12.cloned.1.call-update) | async-done | bytes 167952 | tf_op jit(solution)/shard_map/reduce_scatter | solution.py:177
  391.1 84.0 %reduce-scatter.14.cloned.1.call-done = bf16[64,1312]{1,0:T(8,128)(2,1)} async-done(((bf16[1024,1312]{1,0:T(8,128)(2,1)}), bf16[64,1312]{1,0:T(8,128)(2,1)}) %reduce-scatter.14.cloned.1.call-update) | async-done | bytes 167952 | tf_op jit(solution)/shard_map/reduce_scatter | solution.py:177
  475.2 1.8 pad_maximum_fusion.2
  477.2 3.0 pad_maximum_fusion.1
  480.3 15.1 %all_to_all.61 = bf16[3,1024,1,128]{3,0,2,1:T(4,128)(2,1)S(1)} all-to-all(bf16[3,1024,1,128]{3,0,2,1:T(4,128)(2,1)S(1)} %pad_maximum_fusion.1), channel_id=1, replica_groups=mesh['dp'=4,'ctx'=4,'tensor'=2] {'ctx'}, dimensions={1} | all-to-all | bytes 1572864 | tf_op jit(solution)/shard_map/all_to_all | solution.py:207
  497.7 1.9 pad_maximum_fusion
  499.6 4.7 copy.205
  506.1 3.2 fusion.20
  509.3 1.9 collective-permute-done.3
  511.8 38.5 %psum.7 = f32[2,1024]{1,0:T(2,128)S(1)} all-reduce(f32[2,1024]{1,0:T(2,128)S(1)} %pad_maximum_fusion.4), channel_id=1, replica_groups=mesh['dp'=4,'ctx'=4,'tensor'=2] {'dp','ctx'}, use_global_device_ids=true, to_apply=%region_16.17 | all-reduce | flops 2048 | bytes 16384 | tf_op jit(solution)/shard_map/psum | solution.py:222
  552.4 1.5 reduce-scatter.10.cloned.1.call-done
  553.9 9.5 %all_gather.33 = bf16[256,512]{1,0:T(8,128)(2,1)S(1)} all-gather(bf16[64,512]{1,0:T(8,128)(2,1)} %reduce-scatter.10.cloned.1.call-done), channel_id=1, replica_groups=mesh['dp'=4,'ctx'=4,'tensor'=2] {'ctx'}, dimensions={0}, use_global_device_ids=true | all-gather | bytes 327680 | tf_op jit(solution)/shard_map/all_gather | solution.py:227
  564.4 72.0 %reduce-scatter.18.cloned.1.call-done = bf16[64,1312]{1,0:T(8,128)(2,1)} async-done(((bf16[1024,1312]{1,0:T(8,128)(2,1)}), bf16[64,1312]{1,0:T(8,128)(2,1)}) %reduce-scatter.18.cloned.1.call-update) | async-done | bytes 167952 | tf_op jit(solution)/shard_map/reduce_scatter | solution.py:166
  636.4 11.9 %all_gather.35 = bf16[256,1312]{1,0:T(8,128)(2,1)S(1)} all-gather(bf16[64,1312]{1,0:T(8,128)(2,1)} %reduce-scatter.18.cloned.1.call-done), channel_id=1, replica_groups=mesh['dp'=4,'ctx'=4,'tensor'=2] {'ctx'}, dimensions={0}, use_global_device_ids=true | all-gather | bytes 839680 | tf_op jit(solution)/shard_map/all_gather | solution.py:225
  648.4 1.5 copy.198
  649.9 15.7 %all-gather.14.cloned.1.call-done = bf16[2,256,1312]{2,1,0:T(8,128)(2,1)} async-done(((bf16[2,64,1312]{2,1,0:T(8,128)(2,1)}), bf16[2,256,1312]{2,1,0:T(8,128)(2,1)}) %all-gather.14.cloned.1.call-update) | async-done | bytes 1343504 | tf_op jit(solution)/shard_map/all_gather | solution.py:226
  665.6 3.0 copy.197
  668.5 134.2 %reduce-scatter.16.cloned.1.call-done = bf16[64,1536]{1,0:T(8,128)(2,1)} async-done(((bf16[1024,1536]{1,0:T(8,128)(2,1)}), bf16[64,1536]{1,0:T(8,128)(2,1)}) %reduce-scatter.16.cloned.1.call-update) | async-done | bytes 196624
  804.1 12.0 %all_gather.32 = bf16[3,256,512]{2,1,0:T(8,128)(2,1)S(1)} all-gather(bf16[3,64,512]{2,1,0:T(8,128)(2,1)S(1)} %bitcast.158), channel_id=1, replica_groups=mesh['dp'=4,'ctx'=4,'tensor'=2] {'ctx'}, dimensions={1}, use_global_device_ids=true | all-gather | bytes 983040 | tf_op jit(solution)/shard_map/all_gather | solution.py:228
  (159 shorter events, 42.1 us)
Async XLA Ops:
  7.2 3.8 copy-start
  7.2 5.1 copy-start.20
  7.2 6.2 copy-start.22
  7.2 6.4 copy-start.23
  7.2 6.3 copy-start.24
  7.2 6.4 copy-start.4
  7.2 74.8 %all-gather.6.cloned.1.call-start = ((), (), s32[]{:S(2)}) async-start(), calls=%async_computation.9 | async-start | bytes 3342336 | tf_op jit(solution)/shard_map/all_gather | solution.py:125
  9.1 132.7 %all-gather.8.cloned.1.call-start = ((), (), s32[]{:S(2)}) async-start(), calls=%async_computation.10 | async-start | bytes 1114112 | tf_op jit(solution)/shard_map/all_gather | solution.py:126
  10.9 221.9 %all-gather.10.cloned.1.call-start = ((), (), s32[]{:S(2)}) async-start(), calls=%async_computation.11 | async-start | bytes 6127616 | tf_op jit(solution)/shard_map/all_gather | solution.py:127
  12.2 287.9 %all-gather.12.cloned.1.call-start = ((), (), s32[]{:S(2)}) async-start(), calls=%async_computation.12 | async-start | bytes 3063808 | tf_op jit(solution)/shard_map/all_gather | solution.py:128
  85.9 13.1 %all-to-all-start = ((bf16[3,256,4,128]{1,3,0,2:T(8,128)(2,1)}), bf16[3,256,4,128]{1,3,0,2:T(8,128)(2,1)S(1)}, u32[]{:S(2)}, u32[]{:S(2)}) async-start(bf16[3,256,4,128]{1,3,0,2:T(8,128)(2,1)} %copy.170), calls=%async_computation | async-start | bytes 1572864 | tf_op jit(solution)/shard_map/all_to_all | solution.py:143
  89.5 301.7 %reduce-scatter.12.cloned.1.call-start = ((), (), s32[]{:S(2)}) async-start(), calls=%async_computation.14 | async-start | bytes 3063808 | tf_op jit(solution)/shard_map/reduce_scatter | solution.py:177
  90.6 13.7 %copy-start.9 = (f32[1024,64]{0,1:T(8,128)}, f32[1024,64]{0,1:T(8,128)S(1)}, u32[]{:S(2)}) copy-start(f32[1024,64]{0,1:T(8,128)S(1)} %get-tuple-element.105) | copy-start | bytes 786436
  91.2 19.4 %copy-start.6 = (pred[1024,1024]{0,1:T(8,128)(4,1)}, pred[1024,1024]{0,1:T(8,128)(4,1)S(1)}, u32[]{:S(2)}) copy-start(pred[1024,1024]{0,1:T(8,128)(4,1)S(1)} %broadcast_compare_fusion) | copy-start | bytes 3145732
  104.2 1.1 copy-start.17
  105.3 3.3 copy-start.12
  105.7 5.0 copy-start.19
  108.6 4.8 copy-start.5
  113.5 10.3 %copy-start.15 = (bf16[2,64,1024]{2,1,0:T(8,128)(2,1)}, bf16[2,64,1024]{2,1,0:T(8,128)(2,1)S(1)}, u32[]{:S(2)}) copy-start(bf16[2,64,1024]{2,1,0:T(8,128)(2,1)S(1)} %fusion.27) | copy-start | bytes 786436
  143.6 2.0 collective-permute-start
  232.8 67.3 %copy-start.11 = (bf16[256,1024]{1,0:T(8,128)(2,1)S(1)}, bf16[256,1024]{1,0:T(8,128)(2,1)}, u32[]{:S(2)}) copy-start(bf16[256,1024]{1,0:T(8,128)(2,1)} %param.17) | copy-start | bytes 1572868
  305.0 0.8 copy-start.18
  305.0 12.7 %copy-start.8 = (bf16[256,1312]{0,1:T(8,128)(2,1)}, bf16[256,1312]{0,1:T(8,128)(2,1)S(1)}, u32[]{:S(2)}) copy-start(bf16[256,1312]{0,1:T(8,128)(2,1)S(1)} %get-tuple-element.82) | copy-start | bytes 2015236
  308.6 166.5 %reduce-scatter.14.cloned.1.call-start = ((), (), s32[]{:S(2)}) async-start(), calls=%async_computation.15 | async-start | bytes 3063808 | tf_op jit(solution)/shard_map/reduce_scatter | solution.py:177
  312.6 241.3 %reduce-scatter.10.cloned.1.call-start = ((), (), s32[]{:S(2)}) async-start(), calls=%async_computation.13 | async-start | bytes 1114112 | tf_op jit(solution)/shard_map/reduce_scatter | solution.py:187
  312.6 5.1 copy-start.21
  317.6 2.0 collective-permute-start.2
  318.8 2.1 collective-permute-start.1
  322.1 1.0 copy-start.2
  324.6 311.9 %reduce-scatter.18.cloned.1.call-start = ((), (), s32[]{:S(2)}) async-start(), calls=%async_computation.18 | async-start | bytes 3063808 | tf_op jit(solution)/shard_map/reduce_scatter | solution.py:166
  329.8 1.2 copy-start.3
  329.8 17.2 %copy-start.7 = (pred[1024,1024]{0,1:T(8,128)(4,1)S(1)}, pred[1024,1024]{0,1:T(8,128)(4,1)}, u32[]{:S(2)}) copy-start(pred[1024,1024]{0,1:T(8,128)(4,1)} %copy-done.6) | copy-start | bytes 3145732
  333.6 13.0 %all-to-all-start.2 = ((bf16[256,4,128]{0,2,1:T(8,128)(2,1)}), bf16[256,4,128]{0,2,1:T(8,128)(2,1)S(1)}, u32[]{:S(2)}, u32[]{:S(2)}) async-start(bf16[256,4,128]{0,2,1:T(8,128)(2,1)} %bitcast.26), calls=%async_computation.2 | async-start | bytes 524288 | tf_op jit(solution)/shard_map/all_to_all | solution.py:191
  337.0 328.5 %all-gather.14.cloned.1.call-start = ((), (), s32[]{:S(2)}) async-start(), calls=%async_computation.16 | async-start | bytes 1802240 | tf_op jit(solution)/shard_map/all_gather | solution.py:226
  347.0 6.6 copy-start.16
  356.0 6.8 copy-start.14
  362.9 1.4 copy-start.13
  364.3 1.0 copy-start.10
  477.0 325.7 %reduce-scatter.16.cloned.1.call-start = ((), (), s32[]{:S(2)}) async-start(), calls=%async_computation.17 | async-start | bytes 3342336
  509.3 2.0 collective-permute-start.3
  665.5 151.9 %copy-start.1 = (bf16[2,256,1312]{1,2,0:T(8,128)(2,1)S(1)}, bf16[2,256,1312]{1,2,0:T(8,128)(2,1)}, u32[]{:S(2)}) copy-start(bf16[2,256,1312]{1,2,0:T(8,128)(2,1)} %param.15) | copy-start | bytes 4030468
Sparse Core Ops, SparseCore 0:
  11.4 70.5 all-gather.5
  85.3 56.4 all-gather.7
  145.2 87.6 all-gather.9
  235.4 64.6 all-gather.11
  308.8 82.3 reduce-scatter.11
  393.3 81.8 reduce-scatter.13
  478.0 75.8 reduce-scatter.9
  556.2 80.2 reduce-scatter.17
  638.9 26.6 all-gather.13
  670.4 132.3 reduce-scatter.15
where the time goes:
time: 833 us; the launch traced here: 825 us
  waiting for transfers between devices  574 us (69%)
  blocking collectives  108 us (13%)
  matrix products  59.8 us (7%)
  local copies, waits for them, and re-layouts  37.5 us (5%)
  other arithmetic  21.4 us (3%)
  between operations  15.1 us (2%)
  starting transfers between devices  8.46 us (1%)
    unnamed x11, waiting for transfers between devices  134 us
    reduce_scatter x2, waiting for transfers between devices, local(): lax.psum_scatter(grad_in[k].astype(bf16), BOTH, scatter_dimension=0, tile...  107 us
    all_gather x1, waiting for transfers between devices, local(): w_in_all = lax.all_gather(own_rows(w_in, 1), BOTH, axis=1, tiled=True)  86.8 us
    reduce_scatter x1, waiting for transfers between devices, local(): lax.psum_scatter(grad_mlp_out.astype(bf16), BOTH, scatter_dimension=0, ti...  72 us
    all_gather x1, waiting for transfers between devices, local(): lax.all_gather(own_rows(w_mlp_out.T, 0), BOTH, axis=0, tiled=True)  61.3 us
    all_gather x1, waiting for transfers between devices, local(): w_query_all = lax.all_gather(own_rows(w_qkv, 1), BOTH, axis=1, tiled=True)  55.1 us
    psum x1, blocking collectives, local(): gain_sums = lax.psum(jnp.stack([grad_gain_attn, grad_gain_mlp]), BOTH)  38.5 us
    unnamed x63, local copies, waits for them, and re-layouts  20.4 us
  transfers between devices with their start and end apart: 16, of which 16 were waited for; matrix products, arithmetic and copies ran while one was open for 13% of the time, Pallas kernels for 0%

commit v1 on v0

--- a/solution.py
+++ b/solution.py
@@ -10,6 +10,11 @@
 MASK_FILL = -1e30
 INV_ROOT_TWO = 1.0 / math.sqrt(2.0)
 INV_ROOT_TWO_PI = 1.0 / math.sqrt(2.0 * math.pi)
+
+
+def map_the_shelves(obj, along_axis):
+    arr_next = lax.all_gather(obj, along_axis).sum(axis=0)
+    return arr_next
 
 
 def norm_forward(x_float, gain_vec):
@@ -219,7 +224,7 @@
     )
     back_one, grad_gain_attn = norm_backward(grad_normed_one, hat_one, inv_one, gain_one)
     grad_tok = grad_mixed + back_one
-    gain_sums = lax.psum(jnp.stack([grad_gain_attn, grad_gain_mlp]), BOTH)
+    gain_sums = map_the_shelves(jnp.stack([grad_gain_attn, grad_gain_mlp]), BOTH)
     gain_rows = gain_attn.shape[0]
     gain_own = lax.dynamic_slice_in_dim(gain_sums, lax.axis_index("dp") * gain_rows, gain_rows, 1)
     own_down = lax.all_gather(share_down, "ctx", axis=0, tiled=True).astype(f32).T

time: 833 us -> 834 us (level)
    psum x1 -> x0, blocking collectives: 38.5 us -> none  [local(): gain_sums = lax.psum(jnp.stack([grad_gain_attn, grad_gain_mlp]), BOTH)]
    all_gather x0 -> x1, blocking collectives: none -> 37.7 us  [map_the_shelves(): arr_next = lax.all_gather(obj, along_axis).sum(axis=0)]
where the time goes in v1:
time: 834 us; the launch traced here: 825 us
  waiting for transfers between devices  576 us (69%)
  blocking collectives  106 us (13%)
  matrix products  59.8 us (7%)
  local copies, waits for them, and re-layouts  37.5 us (4%)
  other arithmetic  21.5 us (3%)
  between operations  15.1 us (2%)
  starting transfers between devices  8.46 us (1%)
    unnamed x11, waiting for transfers between devices  134 us
    reduce_scatter x2, waiting for transfers between devices, local(): lax.psum_scatter(grad_in[k].astype(bf16), BOTH, scatter_dimension=0, tile...  107 us
    all_gather x1, waiting for transfers between devices, local(): w_in_all = lax.all_gather(own_rows(w_in, 1), BOTH, axis=1, tiled=True)  86.8 us
    reduce_scatter x1, waiting for transfers between devices, local(): lax.psum_scatter(grad_mlp_out.astype(bf16), BOTH, scatter_dimension=0, ti...  71.9 us
    all_gather x1, waiting for transfers between devices, local(): lax.all_gather(own_rows(w_mlp_out.T, 0), BOTH, axis=0, tiled=True)  61.3 us
    all_gather x1, waiting for transfers between devices, local(): w_query_all = lax.all_gather(own_rows(w_qkv, 1), BOTH, axis=1, tiled=True)  55.1 us
    all_gather x1, blocking collectives, map_the_shelves(): arr_next = lax.all_gather(obj, along_axis).sum(axis=0)  37.7 us
    unnamed x63, local copies, waits for them, and re-layouts  20.4 us
  transfers between devices with their start and end apart: 16, of which 16 were waited for; matrix products, arithmetic and copies ran while one was open for 13% of the time, Pallas kernels for 0%

profile of v1, /device:TPU:0, one launch (start us, length us, event | category | flops | bytes accessed | tf_op | source)
XLA Modules:
  0.0 824.8 jit_solution(11328688421913101839)
XLA Ops:
  7.3 1.8 constant_dynamic-slice_fusion.4
  14.1 12.7 %all_gather.34 = bf16[2,1024]{1,0:T(2,128)(2,1)S(1)} all-gather(bf16[2,256]{1,0:T(2,128)(2,1)S(1)} %pad_maximum_fusion.4), channel_id=1, replica_groups=mesh['dp'=4,'ctx'=4,'tensor'=2] {'dp'}, dimensions={1}, use_global_device_ids=true | all-gather | bytes 5120 | tf_op jit(solution)/shard_map/all_gather | solution.py:128
  26.9 55.1 %all-gather.8.cloned.1.call-done = bf16[3,1024,512]{2,1,0:T(8,128)(2,1)} async-done(((bf16[3,64,512]{2,1,0:T(8,128)(2,1)}), bf16[3,1024,512]{2,1,0:T(8,128)(2,1)}) %all-gather.8.cloned.1.call-update) | async-done | bytes 3145744 | tf_op jit(solution)/shard_map/all_gather | solution.py:130
  82.0 3.0 convolution_convert_fusion.7
  85.9 3.5 all-to-all-start
  91.2 7.8 all-to-all-done
  100.7 2.2 copy.172
  105.7 2.9 fusion.2
  108.6 2.0 fusion
  110.7 2.8 fusion.27
  115.1 8.7 %all_to_all.60 = bf16[4,2,16384]{2,1,0:T(2,128)(2,1)S(1)} all-to-all(bf16[4,2,16384]{2,1,0:T(2,128)(2,1)S(1)} %reshape.241), channel_id=1, replica_groups=mesh['dp'=4,'ctx'=4,'tensor'=2] {'ctx'}, dimensions={0} | all-to-all | bytes 524288 | tf_op jit(solution)/shard_map/all_to_all | solution.py:154
  124.3 17.6 %all-gather.10.cloned.1.call-done = bf16[1024,512]{1,0:T(8,128)(2,1)} async-done(((bf16[64,512]{1,0:T(8,128)(2,1)}), bf16[1024,512]{1,0:T(8,128)(2,1)}) %all-gather.10.cloned.1.call-update) | async-done | bytes 1048592 | tf_op jit(solution)/shard_map/all_gather | solution.py:131
  141.8 1.7 convolution_convert_fusion.8
  143.6 1.9 collective-permute-done
  146.1 86.8 %all-gather.12.cloned.1.call-done = bf16[2,1024,1312]{2,1,0:T(8,128)(2,1)} async-done(((bf16[2,64,1312]{2,1,0:T(8,128)(2,1)}), bf16[2,1024,1312]{2,1,0:T(8,128)(2,1)}) %all-gather.12.cloned.1.call-update) | async-done | bytes 5373968 | tf_op jit(solution)/shard_map/all_gather | solution.py:132
  232.8 6.0 convolution_bitcast_fusion
  238.9 61.3 %all-gather.14.cloned.1.call-done = bf16[1024,1312]{1,0:T(8,128)(2,1)} async-done(((bf16[64,1312]{1,0:T(8,128)(2,1)}), bf16[1024,1312]{1,0:T(8,128)(2,1)}) %all-gather.14.cloned.1.call-update) | async-done | bytes 2686992 | tf_op jit(solution)/shard_map/all_gather | solution.py:133
  300.2 4.9 fusion.13
  305.9 2.7 convolution_convert_fusion.2
  308.7 3.9 convolution_convert_fusion.1
  312.6 5.0 fusion.17
  323.1 1.5 convolution_convert_fusion.6
  324.8 2.1 fusion.7
  326.9 2.9 copy.207
  331.1 1.7 convolution_convert_fusion.10
  333.6 3.4 all-to-all-start.2
  337.1 9.5 %all-to-all-done.2 = bf16[256,4,128]{0,2,1:T(8,128)(2,1)S(1)} async-done(((bf16[256,4,128]{0,2,1:T(8,128)(2,1)}), bf16[256,4,128]{0,2,1:T(8,128)(2,1)S(1)}, u32[]{:S(2)}, u32[]{:S(2)}) %all-to-all-start.2) | async-done | bytes 262176 | tf_op jit(solution)/shard_map/all_to_all | solution.py:196
  347.0 6.6 fusion.28
  356.1 6.8 multiply_convert_fusion
  367.7 23.4 %reduce-scatter.12.cloned.1.call-done = bf16[64,1312]{1,0:T(8,128)(2,1)} async-done(((bf16[1024,1312]{1,0:T(8,128)(2,1)}), bf16[64,1312]{1,0:T(8,128)(2,1)}) %reduce-scatter.12.cloned.1.call-update) | async-done | bytes 167952 | tf_op jit(solution)/shard_map/reduce_scatter | solution.py:182
  391.1 84.0 %reduce-scatter.14.cloned.1.call-done = bf16[64,1312]{1,0:T(8,128)(2,1)} async-done(((bf16[1024,1312]{1,0:T(8,128)(2,1)}), bf16[64,1312]{1,0:T(8,128)(2,1)}) %reduce-scatter.14.cloned.1.call-update) | async-done | bytes 167952 | tf_op jit(solution)/shard_map/reduce_scatter | solution.py:182
  475.2 1.8 pad_maximum_fusion.2
  477.2 3.0 pad_maximum_fusion.1
  480.3 15.1 %all_to_all.61 = bf16[3,1024,1,128]{3,0,2,1:T(4,128)(2,1)S(1)} all-to-all(bf16[3,1024,1,128]{3,0,2,1:T(4,128)(2,1)S(1)} %pad_maximum_fusion.1), channel_id=1, replica_groups=mesh['dp'=4,'ctx'=4,'tensor'=2] {'ctx'}, dimensions={1} | all-to-all | bytes 1572864 | tf_op jit(solution)/shard_map/all_to_all | solution.py:212
  497.7 1.9 pad_maximum_fusion
  499.6 4.7 copy.205
  506.1 3.2 fusion.20
  509.3 1.9 collective-permute-done.3
  511.8 37.7 %all-gather.1 = f32[16,2,1024]{2,1,0:T(2,128)S(1)} all-gather(f32[1,2,1024]{2,1,0:T(2,128)S(1)} %maximum_bitcast_fusion), channel_id=2, replica_groups=mesh['dp'=4,'ctx'=4,'tensor'=2] {'dp','ctx'}, dimensions={0}, use_global_device_ids=true | all-gather | bytes 139264 | tf_op jit(solution)/shard_map/all_gather | solution.py:16
  551.6 2.2 reduce-scatter.10.cloned.1.call-done
  553.8 9.5 %all_gather.41 = bf16[256,512]{1,0:T(8,128)(2,1)S(1)} all-gather(bf16[64,512]{1,0:T(8,128)(2,1)} %reduce-scatter.10.cloned.1.call-done), channel_id=1, replica_groups=mesh['dp'=4,'ctx'=4,'tensor'=2] {'ctx'}, dimensions={0}, use_global_device_ids=true | all-gather | bytes 327680 | tf_op jit(solution)/shard_map/all_gather | solution.py:232
  564.4 71.9 %reduce-scatter.18.cloned.1.call-done = bf16[64,1312]{1,0:T(8,128)(2,1)} async-done(((bf16[1024,1312]{1,0:T(8,128)(2,1)}), bf16[64,1312]{1,0:T(8,128)(2,1)}) %reduce-scatter.18.cloned.1.call-update) | async-done | bytes 167952 | tf_op jit(solution)/shard_map/reduce_scatter | solution.py:171
  636.2 10.9 %all_gather.43 = bf16[256,1312]{1,0:T(8,128)(2,1)S(1)} all-gather(bf16[64,1312]{1,0:T(8,128)(2,1)} %reduce-scatter.18.cloned.1.call-done), channel_id=1, replica_groups=mesh['dp'=4,'ctx'=4,'tensor'=2] {'ctx'}, dimensions={0}, use_global_device_ids=true | all-gather | bytes 839680 | tf_op jit(solution)/shard_map/all_gather | solution.py:230
  647.2 1.5 copy.198
  648.7 17.2 %all-gather.16.cloned.1.call-done = bf16[2,256,1312]{2,1,0:T(8,128)(2,1)} async-done(((bf16[2,64,1312]{2,1,0:T(8,128)(2,1)}), bf16[2,256,1312]{2,1,0:T(8,128)(2,1)}) %all-gather.16.cloned.1.call-update) | async-done | bytes 1343504 | tf_op jit(solution)/shard_map/all_gather | solution.py:231
  665.9 3.0 copy.197
  668.8 134.2 %reduce-scatter.16.cloned.1.call-done = bf16[64,1536]{1,0:T(8,128)(2,1)} async-done(((bf16[1024,1536]{1,0:T(8,128)(2,1)}), bf16[64,1536]{1,0:T(8,128)(2,1)}) %reduce-scatter.16.cloned.1.call-update) | async-done | bytes 196624
  804.4 12.0 %all_gather.40 = bf16[3,256,512]{2,1,0:T(8,128)(2,1)S(1)} all-gather(bf16[3,64,512]{2,1,0:T(8,128)(2,1)S(1)} %bitcast.160), channel_id=1, replica_groups=mesh['dp'=4,'ctx'=4,'tensor'=2] {'ctx'}, dimensions={1}, use_global_device_ids=true | all-gather | bytes 983040 | tf_op jit(solution)/shard_map/all_gather | solution.py:233
  (160 shorter events, 42.1 us)
Async XLA Ops:
  7.2 3.8 copy-start
  7.2 5.1 copy-start.20
  7.2 6.2 copy-start.22
  7.2 6.4 copy-start.23
  7.2 6.3 copy-start.24
  7.2 6.4 copy-start.4
  7.2 74.8 %all-gather.8.cloned.1.call-start = ((), (), s32[]{:S(2)}) async-start(), calls=%async_computation.9 | async-start | bytes 3342336 | tf_op jit(solution)/shard_map/all_gather | solution.py:130
  9.1 132.7 %all-gather.10.cloned.1.call-start = ((), (), s32[]{:S(2)}) async-start(), calls=%async_computation.10 | async-start | bytes 1114112 | tf_op jit(solution)/shard_map/all_gather | solution.py:131
  10.9 221.9 %all-gather.12.cloned.1.call-start = ((), (), s32[]{:S(2)}) async-start(), calls=%async_computation.11 | async-start | bytes 6127616 | tf_op jit(solution)/shard_map/all_gather | solution.py:132
  12.2 287.9 %all-gather.14.cloned.1.call-start = ((), (), s32[]{:S(2)}) async-start(), calls=%async_computation.12 | async-start | bytes 3063808 | tf_op jit(solution)/shard_map/all_gather | solution.py:133
  85.9 13.1 %all-to-all-start = ((bf16[3,256,4,128]{1,3,0,2:T(8,128)(2,1)}), bf16[3,256,4,128]{1,3,0,2:T(8,128)(2,1)S(1)}, u32[]{:S(2)}, u32[]{:S(2)}) async-start(bf16[3,256,4,128]{1,3,0,2:T(8,128)(2,1)} %copy.170), calls=%async_computation | async-start | bytes 1572864 | tf_op jit(solution)/shard_map/all_to_all | solution.py:148
  89.5 301.7 %reduce-scatter.12.cloned.1.call-start = ((), (), s32[]{:S(2)}) async-start(), calls=%async_computation.14 | async-start | bytes 3063808 | tf_op jit(solution)/shard_map/reduce_scatter | solution.py:182
  90.6 13.7 %copy-start.9 = (f32[1024,64]{0,1:T(8,128)}, f32[1024,64]{0,1:T(8,128)S(1)}, u32[]{:S(2)}) copy-start(f32[1024,64]{0,1:T(8,128)S(1)} %get-tuple-element.105) | copy-start | bytes 786436
  91.2 19.4 %copy-start.6 = (pred[1024,1024]{0,1:T(8,128)(4,1)}, pred[1024,1024]{0,1:T(8,128)(4,1)S(1)}, u32[]{:S(2)}) copy-start(pred[1024,1024]{0,1:T(8,128)(4,1)S(1)} %broadcast_compare_fusion) | copy-start | bytes 3145732
  104.2 1.1 copy-start.17
  105.3 3.3 copy-start.12
  105.7 5.0 copy-start.19
  108.6 4.8 copy-start.5
  113.5 10.3 %copy-start.15 = (bf16[2,64,1024]{2,1,0:T(8,128)(2,1)}, bf16[2,64,1024]{2,1,0:T(8,128)(2,1)S(1)}, u32[]{:S(2)}) copy-start(bf16[2,64,1024]{2,1,0:T(8,128)(2,1)S(1)} %fusion.27) | copy-start | bytes 786436
  143.6 2.0 collective-permute-start
  232.8 67.3 %copy-start.11 = (bf16[256,1024]{1,0:T(8,128)(2,1)S(1)}, bf16[256,1024]{1,0:T(8,128)(2,1)}, u32[]{:S(2)}) copy-start(bf16[256,1024]{1,0:T(8,128)(2,1)} %param.17) | copy-start | bytes 1572868
  305.0 0.8 copy-start.18
  305.0 12.7 %copy-start.8 = (bf16[256,1312]{0,1:T(8,128)(2,1)}, bf16[256,1312]{0,1:T(8,128)(2,1)S(1)}, u32[]{:S(2)}) copy-start(bf16[256,1312]{0,1:T(8,128)(2,1)S(1)} %get-tuple-element.82) | copy-start | bytes 2015236
  308.6 166.5 %reduce-scatter.14.cloned.1.call-start = ((), (), s32[]{:S(2)}) async-start(), calls=%async_computation.15 | async-start | bytes 3063808 | tf_op jit(solution)/shard_map/reduce_scatter | solution.py:182
  312.6 241.3 %reduce-scatter.10.cloned.1.call-start = ((), (), s32[]{:S(2)}) async-start(), calls=%async_computation.13 | async-start | bytes 1114112 | tf_op jit(solution)/shard_map/reduce_scatter | solution.py:192
  312.6 5.1 copy-start.21
  317.6 2.0 collective-permute-start.2
  318.8 2.1 collective-permute-start.1
  322.1 1.0 copy-start.2
  324.6 311.7 %reduce-scatter.18.cloned.1.call-start = ((), (), s32[]{:S(2)}) async-start(), calls=%async_computation.18 | async-start | bytes 3063808 | tf_op jit(solution)/shard_map/reduce_scatter | solution.py:171
  329.8 1.2 copy-start.3
  329.8 17.2 %copy-start.7 = (pred[1024,1024]{0,1:T(8,128)(4,1)S(1)}, pred[1024,1024]{0,1:T(8,128)(4,1)}, u32[]{:S(2)}) copy-start(pred[1024,1024]{0,1:T(8,128)(4,1)} %copy-done.6) | copy-start | bytes 3145732
  333.6 13.0 %all-to-all-start.2 = ((bf16[256,4,128]{0,2,1:T(8,128)(2,1)}), bf16[256,4,128]{0,2,1:T(8,128)(2,1)S(1)}, u32[]{:S(2)}, u32[]{:S(2)}) async-start(bf16[256,4,128]{0,2,1:T(8,128)(2,1)} %bitcast.26), calls=%async_computation.2 | async-start | bytes 524288 | tf_op jit(solution)/shard_map/all_to_all | solution.py:196
  337.0 328.8 %all-gather.16.cloned.1.call-start = ((), (), s32[]{:S(2)}) async-start(), calls=%async_computation.16 | async-start | bytes 1802240 | tf_op jit(solution)/shard_map/all_gather | solution.py:231
  347.0 6.6 copy-start.16
  356.0 6.8 copy-start.14
  362.9 1.4 copy-start.13
  364.3 1.0 copy-start.10
  477.0 326.1 %reduce-scatter.16.cloned.1.call-start = ((), (), s32[]{:S(2)}) async-start(), calls=%async_computation.17 | async-start | bytes 3342336
  509.3 2.0 collective-permute-start.3
  665.9 151.9 %copy-start.1 = (bf16[2,256,1312]{1,2,0:T(8,128)(2,1)S(1)}, bf16[2,256,1312]{1,2,0:T(8,128)(2,1)}, u32[]{:S(2)}) copy-start(bf16[2,256,1312]{1,2,0:T(8,128)(2,1)} %param.15) | copy-start | bytes 4030468
Sparse Core Ops, SparseCore 0:
  11.4 70.5 all-gather.7
  85.3 56.4 all-gather.9
  145.2 87.6 all-gather.11
  235.4 64.6 all-gather.13
  308.8 82.3 reduce-scatter.11
  393.3 81.8 reduce-scatter.13
  478.0 75.7 reduce-scatter.9
  556.1 80.0 reduce-scatter.17
  638.7 27.1 all-gather.15
  670.7 132.3 reduce-scatter.15
